TPU v7x, 32 devices: a whole 2x2x4 slice. The times are simulated.
32 devices in a mesh: case: 2 (over y), panel: 4 (over z), slab: 2 (over x), obs: 2 (over core).
Axes of the slice: x: 2, y: 2, z: 4, core: 2. Of those that a mesh axis runs over, the one named last changes fastest.
Arguments:
- loading: bfloat16 [65536, 512], P(('case', 'panel'), 'slab'), parts along dimension 0, may hold values from -6 to 6
- green: bfloat16 [128, 32768], P(('case', 'obs'), 'panel'), parts along dimension 0, may hold values from -0.03125 to 0.03125
- delays: int32 [128, 2048], P(('case', 'obs'), 'panel'), parts along dimension 0, may hold values from 0 to 120
- offsets: int32 [128, 2048], P(('case', 'obs'), 'panel'), parts along dimension 0, may hold values from 0 to 7
- live_groups: int32 [8], P('case'), parts along dimension 0, may hold values from 1 to 4, as said below
Outputs:
- signal: float32 [128, 512], P(('case', 'obs'), 'slab'), parts along dimension 0
There are 2 independent parts, one for each index of `case`. A program takes and returns all parts, laid end to end along the dimension named above; each array names one. Nothing has to cross between parts.
Inputs may be any that keep to these rules, and one draw needn't show every extreme that they name: `live_groups`: in every draw some sector has all 4 groups live while the sector 4/2 positions away has one.
All inputs are finite; a program needn't handle non-finite values.
Results may differ from a plain program's by a relative error of at most 0.0034.
Values may be sent and summed in bfloat16 or wider, within the bound.
A program may use at most 64 MiB of HBM per device.

v0:
```python
import functools
import math

import jax
import jax.numpy as jnp
from jax import lax
from jax.experimental import pallas as pl
from jax.experimental.pallas import tpu as pltpu
from jax.sharding import PartitionSpec as P

BP = 16
GB = 128
LAGS = 128
TAPS = 8
KT = 256
LANES = 128
ROWS = 8
SHARES = (2, 6, 8, 16)
UNROLL = 8
MESH = pl.DeviceIdType.MESH


def kernel(panels, slabs, live_hbm, load_hbm, green_hbm, delay_hbm, offset_hbm, out_ref,
           live_ref, load_ref, green_in, delay_ref, offset_ref, weight_ref, block_ref, part_ref,
           main_out, tail_out, main_in, tail_in, load_sem, green_sem, small_sem, main_send, main_recv, tail_send, tail_recv):
    panel = lax.axis_index("panel")
    slab = lax.axis_index("slab")
    n_panels, samples = load_hbm.shape
    observers = green_hbm.shape[0]
    blocks = delay_hbm.shape[1]
    chunks = observers // ROWS
    tiles = n_panels // KT
    edges = [tiles * sum(SHARES[:c]) // sum(SHARES) for c in range(len(SHARES) + 1)]
    has_next = slab < slabs - 1
    has_prev = slab > 0

    smalls = [pltpu.make_async_copy(src, dst, small_sem.at[i]) for i, (src, dst) in enumerate(
        ((delay_hbm, delay_ref), (offset_hbm, offset_ref), (live_hbm, live_ref)))]
    loads, greens = [], []
    for c in range(len(SHARES)):
        rows = pl.ds(edges[c] * KT, (edges[c + 1] - edges[c]) * KT)
        greens.append(pltpu.make_async_copy(green_hbm.at[:, rows], green_in.at[:, rows], green_sem.at[c]))
        greens[-1].start()
        loads.append(pltpu.make_async_copy(load_hbm.at[rows, :], load_ref.at[rows, :], load_sem.at[c]))
        loads[-1].start()
    for copy in smalls:
        copy.start()

    barrier = pltpu.get_barrier_semaphore()
    for d in range(1, panels):
        pl.semaphore_signal(barrier, inc=1, device_id={"panel": lax.rem(panel + d, panels)}, device_id_type=MESH)

    @pl.when(has_next)
    def _():
        for d in range(panels):
            pl.semaphore_signal(barrier, inc=1, device_id={
                "panel": lax.rem(panel + d, panels), "slab": slab + 1}, device_id_type=MESH)

    @pl.when(has_prev)
    def _():
        for d in range(panels):
            pl.semaphore_signal(barrier, inc=1, device_id={
                "panel": lax.rem(panel + d, panels), "slab": slab - 1}, device_id_type=MESH)

    block_row = lax.broadcasted_iota(jnp.int32, (BP, KT), 0)
    panel_col = lax.broadcasted_iota(jnp.int32, (BP, KT), 1)
    diagonal = jnp.where(panel_col // BP == block_row, 1.0, 0.0).astype(jnp.bfloat16)

    def tile_step(tile, carry):
        columns = pl.ds(pl.multiple_of(tile * KT, KT), KT)
        pieces = []
        for o in range(observers):
            row = jnp.broadcast_to(green_in[o:o + 1, columns], (BP, KT))
            pieces.append(row * diagonal)
        spread = jnp.concatenate(pieces, axis=0)
        product = jnp.dot(spread, load_ref[columns, :], preferred_element_type=jnp.float32)
        block_ref[:, pl.ds(pl.multiple_of(tile * BP, BP), BP), :] = (
            product.astype(jnp.bfloat16).reshape(observers, BP, samples))
        return carry

    for c in range(len(SHARES)):
        greens[c].wait()
        loads[c].wait()
        lax.fori_loop(edges[c], edges[c + 1], tile_step, 0, unroll=True)

    for copy in smalls:
        copy.wait()
    position = 3.0 + offset_ref[...].astype(jnp.float32) * 0.125
    terms = [position - float(m) for m in range(TAPS)]
    before = [None] * TAPS
    after = [None] * TAPS
    for k in range(1, TAPS):
        before[k] = terms[k - 1] if k == 1 else before[k - 1] * terms[k - 1]
    for k in range(TAPS - 2, -1, -1):
        after[k] = terms[k + 1] if k == TAPS - 2 else after[k + 1] * terms[k + 1]
    for k in range(TAPS):
        scale = 1.0 / math.prod(k - m for m in range(TAPS) if m != k)
        if k == 0:
            value = after[k]
        elif k == TAPS - 1:
            value = before[k]
        else:
            value = before[k] * after[k]
        weight_ref[k] = value * scale
    live = live_ref[panel]
    group_of = lax.broadcasted_iota(jnp.int32, (observers, blocks), 1) // GB
    delay_ref[...] = jnp.where(group_of < live, delay_ref[...], 4 * LAGS)

    sub = lax.broadcasted_iota(jnp.int32, (BP, blocks), 0)
    lane = lax.broadcasted_iota(jnp.int32, (8, LANES), 1)
    row8 = lax.broadcasted_iota(jnp.int32, (8, LANES), 0)
    wide = samples // LANES
    zero = jnp.zeros((8, LANES), jnp.float32)

    def shifted_in(parts, keep):
        return [jnp.where(keep, parts[0], 0.0)] + [
            jnp.where(keep, parts[j], parts[j - 1]) for j in range(1, len(parts))]

    def observer_step(o, carry):
        behind = sub - delay_ref[pl.ds(o, 1), :]
        tap = behind & (BP - 1)
        place = ((BP - 1 - behind) >> 4).astype(jnp.float32).astype(jnp.bfloat16)
        stencil = jnp.zeros((BP, blocks), jnp.float32)
        for k in range(TAPS):
            stencil = jnp.where(tap == k, weight_ref[k, pl.ds(o, 1), :], stencil)
        stencil = stencil.astype(jnp.bfloat16)
        table = jnp.concatenate([
            jnp.where(place == jnp.bfloat16(q), stencil, jnp.bfloat16(0)) for q in range(LAGS // BP)], axis=0)
        lagged = jnp.dot(table, block_ref[o], preferred_element_type=jnp.float32)
        sums = [zero] * (wide + 1)
        for high in range(LAGS // 8):
            shift = 8 * high
            parts = [lagged[shift:shift + 8, j * LANES:(j + 1) * LANES] for j in range(wide)]
            if shift == 0:
                moved = parts + [None]
            else:
                parts = [pltpu.roll(part, shift, 1) for part in parts]
                keep = lane >= shift
                moved = shifted_in(parts, keep) + [jnp.where(keep, 0.0, parts[-1])]
            sums = [a if b is None else a + b for a, b in zip(sums, moved)]
        sums = [pltpu.roll(part, 0, 1, stride=1, stride_axis=0) for part in sums]
        sums = shifted_in(sums, lane >= row8)
        own = row8 == lax.rem(o, ROWS)
        return tuple(
            jnp.where(own, jnp.sum(part, axis=0, keepdims=True), kept) for part, kept in zip(sums, carry))

    def main_copy(c, d):
        return pltpu.make_async_remote_copy(
            src_ref=main_out.at[c],
            dst_ref=main_in.at[c, d - 1],
            send_sem=main_send.at[c, d - 1], recv_sem=main_recv.at[c, d - 1],
            device_id={"panel": lax.rem(panel + d, panels)}, device_id_type=MESH)

    def tail_copy(c, d):
        return pltpu.make_async_remote_copy(
            src_ref=tail_out.at[c],
            dst_ref=tail_in.at[c, d],
            send_sem=tail_send.at[c, d], recv_sem=tail_recv.at[c, d],
            device_id={"panel": lax.rem(panel + d, panels), "slab": slab + 1}, device_id_type=MESH)

    for c in range(chunks):
        gathered = lax.fori_loop(
            c * ROWS, (c + 1) * ROWS, observer_step, (zero,) * (wide + 1), unroll=UNROLL)
        for j in range(wide):
            lanes = slice(j * LANES, (j + 1) * LANES)
            part_ref[c * ROWS:(c + 1) * ROWS, lanes] = gathered[j]
            main_out[c, :, lanes] = gathered[j].astype(jnp.bfloat16)
        tail_out[c] = gathered[wide].astype(jnp.bfloat16)
        if c == 0:
            pl.semaphore_wait(barrier, panels - 1 + panels * (has_next.astype(jnp.int32) + has_prev.astype(jnp.int32)))

        for d in range(1, panels):
            main_copy(c, d).start()

        @pl.when(has_next)
        def _():
            for d in range(panels):
                tail_copy(c, d).start()

    for c in range(chunks):
        rows = slice(c * ROWS, (c + 1) * ROWS)
        total = part_ref[rows, :]
        for d in range(1, panels):
            main_copy(c, d).wait_recv()
            total = total + main_in[c, d - 1].astype(jnp.float32)
        out_ref[rows, :] = total

        @pl.when(has_prev)
        def _():
            late = None
            for d in range(panels):
                tail_copy(c, d).wait_recv()
                term = tail_in[c, d].astype(jnp.float32)
                late = term if late is None else late + term
            out_ref[rows, :LAGS] += late

    for c in range(chunks):
        for d in range(1, panels):
            main_copy(c, d).wait_send()

        @pl.when(has_next)
        def _():
            for d in range(panels):
                tail_copy(c, d).wait_send()


def shards(panels, slabs, loading, green, delays, offsets, live_groups):
    n_panels, samples = loading.shape
    observers = green.shape[0]
    blocks = delays.shape[1]
    chunks = observers // ROWS
    peers = max(panels - 1, 1)
    anywhere = pl.BlockSpec(memory_space=pltpu.HBM)
    return pl.pallas_call(
        functools.partial(kernel, panels, slabs),
        out_shape=jax.ShapeDtypeStruct((observers, samples), jnp.float32),
        in_specs=[anywhere] * 5,
        out_specs=pl.BlockSpec(memory_space=pltpu.VMEM),
        scratch_shapes=[
            pltpu.SMEM((panels,), jnp.int32),
            pltpu.VMEM((n_panels, samples), jnp.bfloat16),
            pltpu.VMEM((observers, n_panels), jnp.bfloat16),
            pltpu.VMEM((observers, blocks), jnp.int32),
            pltpu.VMEM((observers, blocks), jnp.int32),
            pltpu.VMEM((TAPS, observers, blocks), jnp.float32),
            pltpu.VMEM((observers, blocks, samples), jnp.bfloat16),
            pltpu.VMEM((observers, samples), jnp.float32),
            pltpu.VMEM((chunks, ROWS, samples), jnp.bfloat16),
            pltpu.VMEM((chunks, ROWS, LAGS), jnp.bfloat16),
            pltpu.VMEM((chunks, peers, ROWS, samples), jnp.bfloat16),
            pltpu.VMEM((chunks, panels, ROWS, LAGS), jnp.bfloat16),
            pltpu.SemaphoreType.DMA((len(SHARES),)),
            pltpu.SemaphoreType.DMA((len(SHARES),)),
            pltpu.SemaphoreType.DMA((3,)),
            pltpu.SemaphoreType.DMA((chunks, peers)),
            pltpu.SemaphoreType.DMA((chunks, peers)),
            pltpu.SemaphoreType.DMA((chunks, panels)),
            pltpu.SemaphoreType.DMA((chunks, panels)),
        ],
        compiler_params=pltpu.CompilerParams(
            collective_id=0, has_side_effects=True, vmem_limit_bytes=24 * 2 ** 20),
        name="far_field",
    )(*(pltpu.with_memory_space_constraint(x, pltpu.HBM) for x in (live_groups, loading, green, delays, offsets)))


def solution(mesh):
    placed = (
        P(("case", "panel"), "slab"),
        P(("case", "obs"), "panel"),
        P(("case", "obs"), "panel"),
        P(("case", "obs"), "panel"),
        P("case"),
    )
    return jax.shard_map(
        functools.partial(shards, mesh.shape["panel"], mesh.shape["slab"]),
        mesh=mesh, in_specs=placed, out_specs=P(("case", "obs"), "slab"), check_vma=False,
    )
```

profile of v0, /device:TPU:0, one launch (start us, length us, event | category | flops | bytes accessed | tf_op | source)
XLA Modules:
  0.0 14.9 jit_solution(13283158036729754667)
XLA Ops:
  0.0 14.3 %far_field.1 = f32[32,256]{1,0:T(8,128)S(1)} custom-call(s32[4]{0:T(128)} %live_hbm.1, bf16[8192,256]{1,0:T(8,128)(2,1)} %load_hbm.1, bf16[32,8192]{1,0:T(8,128)(2,1)} %green_hbm.1, s32[32,512]{1,0:T(8,128)} %delay_hbm.1, s32[32,512]{1,0:T(8,128)} %offset_hbm.1), custom_call_target="tpu_custom_call" | custom-call | tf_op jit(solution)/shard_map/far_field/pallas_call | solution.py:214
  14.3 0.6 %copy.7 = f32[32,256]{1,0:T(8,128)} copy(f32[32,256]{1,0:T(8,128)S(1)} %far_field.1) | data formatting | bytes 65536
where the time goes:
time: 15 us; the launch traced here: 14.9 us
  Pallas kernels  14.3 us (95%)
  local copies, waits for them, and re-layouts  0.62 us (4%)
    pallas_call x1, Pallas kernels, shards(): pl.pallas_call(functools.partial(kernel, panels, slabs), out_shape=jax.Sh...  14.3 us
    unnamed x1, local copies, waits for them, and re-layouts  0.62 us

commit v1 on v0

v1 whole, which is shorter than its diff:
```python
import functools
import math

import jax
import jax.numpy as jnp
from jax import lax
from jax.experimental import pallas as pl
from jax.experimental.pallas import tpu as pltpu
from jax.sharding import PartitionSpec as P

BP = 16
GB = 128
LAGS = 128
TAPS = 8
STEPS = 8
KT = 256
LANES = 128
ROWS = 8
SHARES = (4, 28)
BEFORE = 8
MESH = pl.DeviceIdType.MESH


def kernel(panels, slabs, live_hbm, load_hbm, green_hbm, delay_hbm, offset_hbm, out_ref,
           live_ref, load_ref, green_ref, delay_ref, offset_ref, table_ref, block_ref, wide_ref, part_ref,
           main_out, tail_out, main_in, tail_in, load_sem, green_sem, small_sem, main_send, main_recv, tail_send, tail_recv):
    panel = lax.axis_index("panel")
    slab = lax.axis_index("slab")
    n_panels, samples = load_hbm.shape
    observers = green_hbm.shape[0]
    blocks = delay_hbm.shape[1]
    chunks = observers // ROWS
    tiles = n_panels // KT
    wide = samples // LANES
    across = blocks // LANES
    edges = [tiles * sum(SHARES[:c]) // sum(SHARES) for c in range(len(SHARES) + 1)]
    has_next = slab < slabs - 1
    has_prev = slab > 0

    smalls = [pltpu.make_async_copy(src, dst, small_sem.at[i]) for i, (src, dst) in enumerate(
        ((delay_hbm, delay_ref), (offset_hbm, offset_ref), (live_hbm, live_ref)))]
    for copy in smalls:
        copy.start()
    greens, loads = [], []
    for c in range(len(SHARES)):
        rows = pl.ds(edges[c] * KT, (edges[c + 1] - edges[c]) * KT)
        greens.append(pltpu.make_async_copy(green_hbm.at[:, rows], green_ref.at[:, rows], green_sem.at[c]))
        greens[-1].start()
        loads.append(pltpu.make_async_copy(load_hbm.at[rows, :], load_ref.at[rows, :], load_sem.at[c]))
        loads[-1].start()

    barrier = pltpu.get_barrier_semaphore()
    for d in range(1, panels):
        pl.semaphore_signal(barrier, inc=1, device_id={"panel": lax.rem(panel + d, panels)}, device_id_type=MESH)

    @pl.when(has_next)
    def _():
        for d in range(panels):
            pl.semaphore_signal(barrier, inc=1, device_id={
                "panel": lax.rem(panel + d, panels), "slab": slab + 1}, device_id_type=MESH)

    @pl.when(has_prev)
    def _():
        for d in range(panels):
            pl.semaphore_signal(barrier, inc=1, device_id={
                "panel": lax.rem(panel + d, panels), "slab": slab - 1}, device_id_type=MESH)

    lane = lax.broadcasted_iota(jnp.int32, (ROWS, LANES), 1)
    row8 = lax.broadcasted_iota(jnp.int32, (ROWS, LANES), 0)
    lane16 = lax.broadcasted_iota(jnp.int32, (BP, LANES), 1)
    row16 = lax.broadcasted_iota(jnp.int32, (BP, LANES), 0)
    diagonal = jnp.where(lane16 // BP == row16 % ROWS, 1.0, 0.0).astype(jnp.bfloat16)
    empty = jnp.zeros((BP, LANES), jnp.bfloat16)

    position = 3.0 + (lane // TAPS).astype(jnp.float32) * 0.125
    tap_of = lane % TAPS
    choice = jnp.ones((ROWS, LANES), jnp.float32)
    below = jnp.ones((ROWS, LANES), jnp.float32)
    for m in range(TAPS):
        here = tap_of == m
        choice = choice * jnp.where(here, 1.0, position - float(m))
        below = below * jnp.where(here, 1.0, (tap_of - m).astype(jnp.float32))
    choice = choice / below

    for copy in smalls:
        copy.wait()
    live = live_ref[panel]
    group_of = lax.broadcasted_iota(jnp.int32, (observers, blocks), 1) // GB
    delay_ref[...] = jnp.where(group_of < live, delay_ref[...], 4 * LAGS)
    offset_ref[...] = offset_ref[...] * TAPS

    def table_step(o):
        for a in range(across):
            lanes = slice(a * LANES, (a + 1) * LANES)
            delay = jnp.broadcast_to(delay_ref[o:o + 1, lanes], (ROWS, LANES))
            step = jnp.broadcast_to(offset_ref[o:o + 1, lanes], (ROWS, LANES))
            which = step + ((row8 - delay) & (ROWS - 1))
            stencil = jnp.take_along_axis(choice, which, axis=1, mode="promise_in_bounds")
            place = ((delay + (ROWS - 1) - row8) >> 3).astype(jnp.float32)
            place = jnp.concatenate([place, place - 1.0], axis=0).astype(jnp.bfloat16)
            stencil = jnp.concatenate([stencil, stencil], axis=0).astype(jnp.bfloat16)
            for q in range(LAGS // BP):
                table_ref[o, q * BP:(q + 1) * BP, lanes] = jnp.where(
                    place == jnp.bfloat16(2 * q), stencil, jnp.bfloat16(0))

    def widen_step(tile):
        columns = slice(tile * KT, (tile + 1) * KT)
        wide_ref[:, columns] = green_ref[:, columns].astype(jnp.float32)

    def spread_step(first, last, tile):
        pieces = []
        for o in range(first, last, 2):
            for h in range(KT // LANES):
                lanes = slice(tile * KT + h * LANES, tile * KT + (h + 1) * LANES)
                pair = jnp.concatenate([
                    jnp.broadcast_to(wide_ref[i:i + 1, lanes], (ROWS, LANES)) for i in (o, o + 1)], axis=0)
                pair = pair.astype(jnp.bfloat16) * diagonal
                pieces.append(jnp.concatenate([pair if i == h else empty for i in range(KT // LANES)], axis=1))
        product = jnp.dot(jnp.concatenate(pieces, axis=0), load_ref[tile * KT:(tile + 1) * KT, :],
                          preferred_element_type=jnp.float32)
        for o in range(first, last, 2):
            for i in range(2):
                start = (o - first) * BP + i * ROWS
                rows = jnp.concatenate([product[start + h * BP:start + h * BP + ROWS] for h in range(KT // LANES)], axis=0)
                block_ref[o + i, tile * BP:(tile + 1) * BP, :] = rows.astype(jnp.bfloat16)

    def lag_step(o):
        return jnp.dot(table_ref[o], block_ref[o], preferred_element_type=jnp.float32)

    def shift(parts, amount):
        keep = lane >= amount
        rolled = [None if part is None else pltpu.roll(part, amount, 1) for part in parts]
        moved = [jnp.where(keep, rolled[0], 0.0)]
        for j in range(1, len(parts)):
            moved.append(jnp.where(keep, 0.0 if rolled[j] is None else rolled[j], rolled[j - 1]))
        return moved

    def add(left, right):
        return [l if r is None else l + r for l, r in zip(left, right)]

    def fold(lagged):
        total = [lagged[:ROWS, j * LANES:(j + 1) * LANES] for j in range(wide)] + [None]
        for h in range(1, LAGS // ROWS):
            parts = [lagged[h * ROWS:(h + 1) * ROWS, j * LANES:(j + 1) * LANES] for j in range(wide)] + [None]
            total = add(shift(parts, h * ROWS), total)
        return total

    def merge(left, right, bit):
        clear = (row8 & bit) == 0
        stay, move = [], []
        for a, b in zip(left, right):
            stay.append(jnp.where(clear, a, pltpu.roll(b, bit, 0)))
            move.append(jnp.where(clear, pltpu.roll(a, ROWS - bit, 0), b))
        return add(shift(move, bit), stay)

    def gather(folded):
        bit = ROWS // 2
        while len(folded) > 1:
            half = len(folded) // 2
            folded = [merge(folded[i], folded[i + half], bit) for i in range(half)]
            bit //= 2
        return folded[0]

    def main_copy(c, d):
        return pltpu.make_async_remote_copy(
            src_ref=main_out.at[c],
            dst_ref=main_in.at[c, d - 1],
            send_sem=main_send.at[c, d - 1], recv_sem=main_recv.at[c, d - 1],
            device_id={"panel": lax.rem(panel + d, panels)}, device_id_type=MESH)

    def tail_copy(c, d):
        return pltpu.make_async_remote_copy(
            src_ref=tail_out.at[c],
            dst_ref=tail_in.at[c, d],
            send_sem=tail_send.at[c, d], recv_sem=tail_recv.at[c, d],
            device_id={"panel": lax.rem(panel + d, panels), "slab": slab + 1}, device_id_type=MESH)

    def keep(c, gathered):
        for j in range(wide):
            lanes = slice(j * LANES, (j + 1) * LANES)
            part_ref[c * ROWS:(c + 1) * ROWS, lanes] = gathered[j]
            main_out[c, :, lanes] = gathered[j].astype(jnp.bfloat16)
        tail_out[c] = gathered[wide].astype(jnp.bfloat16)

    def send(c):
        @pl.when(has_next)
        def _():
            for d in range(panels):
                tail_copy(c, d).start()

        for d in range(1, panels):
            main_copy(c, d).start()

    cut = observers - ROWS
    built = BEFORE
    for o in range(BEFORE):
        table_step(o)
    for c in range(len(SHARES)):
        greens[c].wait()
        loads[c].wait()
        for tile in range(edges[c], edges[c + 1]):
            widen_step(tile)
            spread_step(0, cut, tile)
            due = BEFORE + (observers - BEFORE) * (tile + 1) // tiles
            for o in range(built, due):
                table_step(o)
            built = due

    folded = []
    done = 0
    for tile in range(tiles):
        spread_step(cut, observers, tile)
        due = cut * (tile + 1) // tiles
        for o in range(done, due):
            folded.append(fold(lag_step(o)))
            if len(folded) == ROWS:
                keep(o // ROWS, gather(folded))
                folded = []
        done = due
    pl.semaphore_wait(barrier, panels - 1 + panels * (has_next.astype(jnp.int32) + has_prev.astype(jnp.int32)))
    for c in range(cut // ROWS):
        send(c)

    keep(chunks - 1, gather([fold(lag_step(o)) for o in range(cut, observers)]))
    send(chunks - 1)

    for c in range(chunks):
        rows = slice(c * ROWS, (c + 1) * ROWS)
        total = part_ref[rows, :]
        for d in range(1, panels):
            main_copy(c, d).wait_recv()
            total = total + main_in[c, d - 1].astype(jnp.float32)
        out_ref[rows, :] = total

        @pl.when(has_prev)
        def _():
            late = None
            for d in range(panels):
                tail_copy(c, d).wait_recv()
                term = tail_in[c, d].astype(jnp.float32)
                late = term if late is None else late + term
            out_ref[rows, :LAGS] += late

    for c in range(chunks):
        for d in range(1, panels):
            main_copy(c, d).wait_send()

        @pl.when(has_next)
        def _():
            for d in range(panels):
                tail_copy(c, d).wait_send()


def shards(panels, slabs, loading, green, delays, offsets, live_groups):
    n_panels, samples = loading.shape
    observers = green.shape[0]
    blocks = delays.shape[1]
    chunks = observers // ROWS
    peers = max(panels - 1, 1)
    anywhere = pl.BlockSpec(memory_space=pltpu.HBM)
    return pl.pallas_call(
        functools.partial(kernel, panels, slabs),
        out_shape=jax.ShapeDtypeStruct((observers, samples), jnp.float32),
        in_specs=[anywhere] * 5,
        out_specs=pl.BlockSpec(memory_space=pltpu.VMEM),
        scratch_shapes=[
            pltpu.SMEM((panels,), jnp.int32),
            pltpu.VMEM((n_panels, samples), jnp.bfloat16),
            pltpu.VMEM((observers, n_panels), jnp.bfloat16),
            pltpu.VMEM((observers, blocks), jnp.int32),
            pltpu.VMEM((observers, blocks), jnp.int32),
            pltpu.VMEM((observers, LAGS, blocks), jnp.bfloat16),
            pltpu.VMEM((observers, blocks, samples), jnp.bfloat16),
            pltpu.VMEM((observers, n_panels), jnp.float32),
            pltpu.VMEM((observers, samples), jnp.float32),
            pltpu.VMEM((chunks, ROWS, samples), jnp.bfloat16),
            pltpu.VMEM((chunks, ROWS, LAGS), jnp.bfloat16),
            pltpu.VMEM((chunks, peers, ROWS, samples), jnp.bfloat16),
            pltpu.VMEM((chunks, panels, ROWS, LAGS), jnp.bfloat16),
            pltpu.SemaphoreType.DMA((len(SHARES),)),
            pltpu.SemaphoreType.DMA((len(SHARES),)),
            pltpu.SemaphoreType.DMA((3,)),
            pltpu.SemaphoreType.DMA((chunks, peers)),
            pltpu.SemaphoreType.DMA((chunks, peers)),
            pltpu.SemaphoreType.DMA((chunks, panels)),
            pltpu.SemaphoreType.DMA((chunks, panels)),
        ],
        compiler_params=pltpu.CompilerParams(
            collective_id=0, has_side_effects=True, vmem_limit_bytes=40 * 2 ** 20),
        name="far_field",
    )(*(pltpu.with_memory_space_constraint(x, pltpu.HBM) for x in (live_groups, loading, green, delays, offsets)))


def solution(mesh):
    placed = (
        P(("case", "panel"), "slab"),
        P(("case", "obs"), "panel"),
        P(("case", "obs"), "panel"),
        P(("case", "obs"), "panel"),
        P("case"),
    )
    return jax.shard_map(
        functools.partial(shards, mesh.shape["panel"], mesh.shape["slab"]),
        mesh=mesh, in_specs=placed, out_specs=P(("case", "obs"), "slab"), check_vma=False,
    )
```

time: 15 us -> 15.1 us (level)
  no operation moved by 1% of the time
where the time goes in v1:
time: 15.1 us; the launch traced here: 15 us
  Pallas kernels  14.4 us (95%)
  local copies, waits for them, and re-layouts  0.62 us (4%)
    pallas_call x1, Pallas kernels, shards(): pl.pallas_call(functools.partial(kernel, panels, slabs), out_shape=jax.Sh...  14.4 us
    unnamed x1, local copies, waits for them, and re-layouts  0.62 us

profile of v1, /device:TPU:0, one launch (start us, length us, event | category | flops | bytes accessed | tf_op | source)
XLA Modules:
  0.0 15.0 jit_solution(2614376763101870973)
XLA Ops:
  0.0 14.4 %far_field.1 = f32[32,256]{1,0:T(8,128)S(1)} custom-call(s32[4]{0:T(128)} %live_hbm.1, bf16[8192,256]{1,0:T(8,128)(2,1)} %load_hbm.1, bf16[32,8192]{1,0:T(8,128)(2,1)} %green_hbm.1, s32[32,512]{1,0:T(8,128)} %delay_hbm.1, s32[32,512]{1,0:T(8,128)} %offset_hbm.1), custom_call_target="tpu_custom_call" | custom-call | tf_op jit(solution)/shard_map/far_field/pallas_call | solution.py:261
  14.4 0.6 %copy.7 = f32[32,256]{1,0:T(8,128)} copy(f32[32,256]{1,0:T(8,128)S(1)} %far_field.1) | data formatting | bytes 65536

commit v2 on v1

--- a/solution.py
+++ b/solution.py
@@ -16,8 +16,9 @@
 KT = 256
 LANES = 128
 ROWS = 8
-SHARES = (4, 28)
-BEFORE = 8
+SHARES = (4, 12, 16)
+TABLES = (8, 8, 8)
+LATE = 8
 MESH = pl.DeviceIdType.MESH
 
 
@@ -29,7 +30,6 @@
     n_panels, samples = load_hbm.shape
     observers = green_hbm.shape[0]
     blocks = delay_hbm.shape[1]
-    chunks = observers // ROWS
     tiles = n_panels // KT
     wide = samples // LANES
     across = blocks // LANES
@@ -90,18 +90,18 @@
     offset_ref[...] = offset_ref[...] * TAPS
 
     def table_step(o):
+        stencils, places = [], []
         for a in range(across):
             lanes = slice(a * LANES, (a + 1) * LANES)
             delay = jnp.broadcast_to(delay_ref[o:o + 1, lanes], (ROWS, LANES))
             step = jnp.broadcast_to(offset_ref[o:o + 1, lanes], (ROWS, LANES))
             which = step + ((row8 - delay) & (ROWS - 1))
-            stencil = jnp.take_along_axis(choice, which, axis=1, mode="promise_in_bounds")
-            place = ((delay + (ROWS - 1) - row8) >> 3).astype(jnp.float32)
-            place = jnp.concatenate([place, place - 1.0], axis=0).astype(jnp.bfloat16)
-            stencil = jnp.concatenate([stencil, stencil], axis=0).astype(jnp.bfloat16)
-            for q in range(LAGS // BP):
-                table_ref[o, q * BP:(q + 1) * BP, lanes] = jnp.where(
-                    place == jnp.bfloat16(2 * q), stencil, jnp.bfloat16(0))
+            stencils.append(jnp.take_along_axis(choice, which, axis=1, mode="promise_in_bounds"))
+            places.append(((delay + (ROWS - 1) - row8) >> 3).astype(jnp.float32))
+        stencil = jnp.concatenate(stencils, axis=1).astype(jnp.bfloat16)
+        place = jnp.concatenate(places, axis=1).astype(jnp.bfloat16)
+        for q in range(LAGS // ROWS):
+            table_ref[o, q * ROWS:(q + 1) * ROWS, :] = jnp.where(place == jnp.bfloat16(q), stencil, jnp.bfloat16(0))
 
     def widen_step(tile):
         columns = slice(tile * KT, (tile + 1) * KT)
@@ -161,75 +161,72 @@
             bit //= 2
         return folded[0]
 
+    spans = ((0, observers - LATE), (observers - LATE, observers))
+
     def main_copy(c, d):
+        rows = slice(*spans[c])
         return pltpu.make_async_remote_copy(
-            src_ref=main_out.at[c],
-            dst_ref=main_in.at[c, d - 1],
+            src_ref=main_out.at[rows],
+            dst_ref=main_in.at[d - 1, rows],
             send_sem=main_send.at[c, d - 1], recv_sem=main_recv.at[c, d - 1],
             device_id={"panel": lax.rem(panel + d, panels)}, device_id_type=MESH)
 
     def tail_copy(c, d):
+        rows = slice(*spans[c])
         return pltpu.make_async_remote_copy(
-            src_ref=tail_out.at[c],
-            dst_ref=tail_in.at[c, d],
+            src_ref=tail_out.at[rows],
+            dst_ref=tail_in.at[d, rows],
             send_sem=tail_send.at[c, d], recv_sem=tail_recv.at[c, d],
             device_id={"panel": lax.rem(panel + d, panels), "slab": slab + 1}, device_id_type=MESH)
 
-    def keep(c, gathered):
+    def sum_rows(first):
+        gathered = gather([fold(lag_step(o)) for o in range(first, first + ROWS)])
+        rows = slice(first, first + ROWS)
         for j in range(wide):
             lanes = slice(j * LANES, (j + 1) * LANES)
-            part_ref[c * ROWS:(c + 1) * ROWS, lanes] = gathered[j]
-            main_out[c, :, lanes] = gathered[j].astype(jnp.bfloat16)
-        tail_out[c] = gathered[wide].astype(jnp.bfloat16)
+            part_ref[rows, lanes] = gathered[j]
+            main_out[rows, lanes] = gathered[j].astype(jnp.bfloat16)
+        tail_out[rows, :] = gathered[wide].astype(jnp.bfloat16)
 
     def send(c):
+        for d in range(1, panels):
+            main_copy(c, d).start()
+
         @pl.when(has_next)
         def _():
             for d in range(panels):
                 tail_copy(c, d).start()
 
-        for d in range(1, panels):
-            main_copy(c, d).start()
-
-    cut = observers - ROWS
-    built = BEFORE
-    for o in range(BEFORE):
-        table_step(o)
+    built = 0
+
+    def tables_step(count):
+        nonlocal built
+        for o in range(built, min(built + count, observers)):
+            table_step(o)
+        built = min(built + count, observers)
+
+    tables_step(TABLES[0])
     for c in range(len(SHARES)):
         greens[c].wait()
         loads[c].wait()
         for tile in range(edges[c], edges[c + 1]):
             widen_step(tile)
-            spread_step(0, cut, tile)
-            due = BEFORE + (observers - BEFORE) * (tile + 1) // tiles
-            for o in range(built, due):
-                table_step(o)
-            built = due
-
-    folded = []
-    done = 0
-    for tile in range(tiles):
-        spread_step(cut, observers, tile)
-        due = cut * (tile + 1) // tiles
-        for o in range(done, due):
-            folded.append(fold(lag_step(o)))
-            if len(folded) == ROWS:
-                keep(o // ROWS, gather(folded))
-                folded = []
-        done = due
-    pl.semaphore_wait(barrier, panels - 1 + panels * (has_next.astype(jnp.int32) + has_prev.astype(jnp.int32)))
-    for c in range(cut // ROWS):
+            spread_step(0, observers, tile)
+        tables_step(TABLES[c + 1] if c + 1 < len(SHARES) else observers)
+
+    for c in range(len(spans)):
+        for first in range(spans[c][0], spans[c][1], ROWS):
+            sum_rows(first)
+        if c == 0:
+            pl.semaphore_wait(barrier, panels - 1 + panels * (has_next.astype(jnp.int32) + has_prev.astype(jnp.int32)))
         send(c)
 
-    keep(chunks - 1, gather([fold(lag_step(o)) for o in range(cut, observers)]))
-    send(chunks - 1)
-
-    for c in range(chunks):
-        rows = slice(c * ROWS, (c + 1) * ROWS)
+    for c in range(len(spans)):
+        rows = slice(*spans[c])
         total = part_ref[rows, :]
         for d in range(1, panels):
             main_copy(c, d).wait_recv()
-            total = total + main_in[c, d - 1].astype(jnp.float32)
+            total = total + main_in[d - 1, rows, :].astype(jnp.float32)
         out_ref[rows, :] = total
 
         @pl.when(has_prev)
@@ -237,11 +234,11 @@
             late = None
             for d in range(panels):
                 tail_copy(c, d).wait_recv()
-                term = tail_in[c, d].astype(jnp.float32)
+                term = tail_in[d, rows, :].astype(jnp.float32)
                 late = term if late is None else late + term
             out_ref[rows, :LAGS] += late
 
-    for c in range(chunks):
+    for c in range(len(spans)):
         for d in range(1, panels):
             main_copy(c, d).wait_send()
 
@@ -255,7 +252,6 @@
     n_panels, samples = loading.shape
     observers = green.shape[0]
     blocks = delays.shape[1]
-    chunks = observers // ROWS
     peers = max(panels - 1, 1)
     anywhere = pl.BlockSpec(memory_space=pltpu.HBM)
     return pl.pallas_call(
@@ -273,17 +269,17 @@
             pltpu.VMEM((observers, blocks, samples), jnp.bfloat16),
             pltpu.VMEM((observers, n_panels), jnp.float32),
             pltpu.VMEM((observers, samples), jnp.float32),
-            pltpu.VMEM((chunks, ROWS, samples), jnp.bfloat16),
-            pltpu.VMEM((chunks, ROWS, LAGS), jnp.bfloat16),
-            pltpu.VMEM((chunks, peers, ROWS, samples), jnp.bfloat16),
-            pltpu.VMEM((chunks, panels, ROWS, LAGS), jnp.bfloat16),
+            pltpu.VMEM((observers, samples), jnp.bfloat16),
+            pltpu.VMEM((observers, LAGS), jnp.bfloat16),
+            pltpu.VMEM((peers, observers, samples), jnp.bfloat16),
+            pltpu.VMEM((panels, observers, LAGS), jnp.bfloat16),
             pltpu.SemaphoreType.DMA((len(SHARES),)),
             pltpu.SemaphoreType.DMA((len(SHARES),)),
             pltpu.SemaphoreType.DMA((3,)),
-            pltpu.SemaphoreType.DMA((chunks, peers)),
-            pltpu.SemaphoreType.DMA((chunks, peers)),
-            pltpu.SemaphoreType.DMA((chunks, panels)),
-            pltpu.SemaphoreType.DMA((chunks, panels)),
+            pltpu.SemaphoreType.DMA((2, peers)),
+            pltpu.SemaphoreType.DMA((2, peers)),
+            pltpu.SemaphoreType.DMA((2, panels)),
+            pltpu.SemaphoreType.DMA((2, panels)),
         ],
         compiler_params=pltpu.CompilerParams(
             collective_id=0, has_side_effects=True, vmem_limit_bytes=40 * 2 ** 20),

time: 15.1 us -> 14 us (0.927)
  Pallas kernels: 14.4 us -> 13.2 us
    pallas_call x1, Pallas kernels: 14.4 us -> 13.2 us  [shards(): pl.pallas_call(functools.partial(kernel, panels, slabs), out_shape=jax.Sh...]
where the time goes in v2:
time: 14 us; the launch traced here: 13.9 us
  Pallas kernels  13.2 us (94%)
  local copies, waits for them, and re-layouts  0.62 us (4%)
    pallas_call x1, Pallas kernels, shards(): pl.pallas_call(functools.partial(kernel, panels, slabs), out_shape=jax.Sh...  13.2 us
    unnamed x1, local copies, waits for them, and re-layouts  0.62 us

profile of v2, /device:TPU:0, one launch (start us, length us, event | category | flops | bytes accessed | tf_op | source)
XLA Modules:
  0.0 13.9 jit_solution(8068932896924636557)
XLA Ops:
  0.0 13.2 %far_field.1 = f32[32,256]{1,0:T(8,128)S(1)} custom-call(s32[4]{0:T(128)} %live_hbm.1, bf16[8192,256]{1,0:T(8,128)(2,1)} %load_hbm.1, bf16[32,8192]{1,0:T(8,128)(2,1)} %green_hbm.1, s32[32,512]{1,0:T(8,128)} %delay_hbm.1, s32[32,512]{1,0:T(8,128)} %offset_hbm.1), custom_call_target="tpu_custom_call" | custom-call | tf_op jit(solution)/shard_map/far_field/pallas_call | solution.py:257
  13.2 0.6 %copy.7 = f32[32,256]{1,0:T(8,128)} copy(f32[32,256]{1,0:T(8,128)S(1)} %far_field.1) | data formatting | bytes 65536

commit v3 on v2

--- a/solution.py
+++ b/solution.py
@@ -17,7 +17,8 @@
 LANES = 128
 ROWS = 8
 SHARES = (4, 12, 16)
-TABLES = (8, 8, 8)
+TABLES = (1, 1, 1, 1)
+EVERY = 99
 LATE = 8
 MESH = pl.DeviceIdType.MESH
 
@@ -89,19 +90,34 @@
     delay_ref[...] = jnp.where(group_of < live, delay_ref[...], 4 * LAGS)
     offset_ref[...] = offset_ref[...] * TAPS
 
+    stored = [o for o in range(observers) if o >= observers - LATE or o % EVERY == 0]
+
+    def entries(o, a):
+        lanes = slice(a * LANES, (a + 1) * LANES)
+        delay = jnp.broadcast_to(delay_ref[o:o + 1, lanes], (ROWS, LANES))
+        step = jnp.broadcast_to(offset_ref[o:o + 1, lanes], (ROWS, LANES))
+        which = step + ((row8 - delay) & (ROWS - 1))
+        stencil = jnp.take_along_axis(choice, which, axis=1, mode="promise_in_bounds")
+        return stencil, ((delay + (ROWS - 1) - row8) >> 3).astype(jnp.float32)
+
     def table_step(o):
-        stencils, places = [], []
-        for a in range(across):
-            lanes = slice(a * LANES, (a + 1) * LANES)
-            delay = jnp.broadcast_to(delay_ref[o:o + 1, lanes], (ROWS, LANES))
-            step = jnp.broadcast_to(offset_ref[o:o + 1, lanes], (ROWS, LANES))
-            which = step + ((row8 - delay) & (ROWS - 1))
-            stencils.append(jnp.take_along_axis(choice, which, axis=1, mode="promise_in_bounds"))
-            places.append(((delay + (ROWS - 1) - row8) >> 3).astype(jnp.float32))
-        stencil = jnp.concatenate(stencils, axis=1).astype(jnp.bfloat16)
-        place = jnp.concatenate(places, axis=1).astype(jnp.bfloat16)
+        parts = [entries(o, a) for a in range(across)]
+        stencil = jnp.concatenate([part[0] for part in parts], axis=1).astype(jnp.bfloat16)
+        place = jnp.concatenate([part[1] for part in parts], axis=1).astype(jnp.bfloat16)
         for q in range(LAGS // ROWS):
             table_ref[o, q * ROWS:(q + 1) * ROWS, :] = jnp.where(place == jnp.bfloat16(q), stencil, jnp.bfloat16(0))
+
+    def table_of(o):
+        if o in stored:
+            return table_ref[o]
+        columns = []
+        for a in range(across):
+            stencil, place = entries(o, a)
+            place = jnp.concatenate([place, place - 1.0], axis=0).astype(jnp.bfloat16)
+            stencil = jnp.concatenate([stencil, stencil], axis=0).astype(jnp.bfloat16)
+            columns.append(jnp.concatenate([
+                jnp.where(place == jnp.bfloat16(2 * q), stencil, jnp.bfloat16(0)) for q in range(LAGS // BP)], axis=0))
+        return jnp.concatenate(columns, axis=1)
 
     def widen_step(tile):
         columns = slice(tile * KT, (tile + 1) * KT)
@@ -125,7 +141,7 @@
                 block_ref[o + i, tile * BP:(tile + 1) * BP, :] = rows.astype(jnp.bfloat16)
 
     def lag_step(o):
-        return jnp.dot(table_ref[o], block_ref[o], preferred_element_type=jnp.float32)
+        return jnp.dot(table_of(o), block_ref[o], preferred_element_type=jnp.float32)
 
     def shift(parts, amount):
         keep = lane >= amount
@@ -138,12 +154,21 @@
     def add(left, right):
         return [l if r is None else l + r for l, r in zip(left, right)]
 
-    def fold(lagged):
-        total = [lagged[:ROWS, j * LANES:(j + 1) * LANES] for j in range(wide)] + [None]
+    def fold(left, right):
+        totals = [[lagged[:ROWS, j * LANES:(j + 1) * LANES] for j in range(wide)] + [None] for lagged in (left, right)]
         for h in range(1, LAGS // ROWS):
-            parts = [lagged[h * ROWS:(h + 1) * ROWS, j * LANES:(j + 1) * LANES] for j in range(wide)] + [None]
-            total = add(shift(parts, h * ROWS), total)
-        return total
+            rows = slice(h * ROWS, (h + 1) * ROWS)
+            keep = lane16 >= h * ROWS
+            rolled = []
+            for j in range(wide):
+                lanes = slice(j * LANES, (j + 1) * LANES)
+                both = jnp.concatenate([left[rows, lanes], right[rows, lanes]], axis=0).astype(jnp.bfloat16)
+                rolled.append(pltpu.roll(both, h * ROWS, 1))
+            none = jnp.zeros_like(rolled[0])
+            moved = [jnp.where(keep, a, b) for a, b in zip(rolled + [none], [none] + rolled)]
+            moved = [part.astype(jnp.float32) for part in moved]
+            totals = [add([part[i * ROWS:(i + 1) * ROWS] for part in moved], totals[i]) for i in range(2)]
+        return totals
 
     def merge(left, right, bit):
         clear = (row8 & bit) == 0
@@ -180,7 +205,10 @@
             device_id={"panel": lax.rem(panel + d, panels), "slab": slab + 1}, device_id_type=MESH)
 
     def sum_rows(first):
-        gathered = gather([fold(lag_step(o)) for o in range(first, first + ROWS)])
+        folded = []
+        for o in range(first, first + ROWS, 2):
+            folded += fold(lag_step(o), lag_step(o + 1))
+        gathered = gather(folded)
         rows = slice(first, first + ROWS)
         for j in range(wide):
             lanes = slice(j * LANES, (j + 1) * LANES)
@@ -197,22 +225,18 @@
             for d in range(panels):
                 tail_copy(c, d).start()
 
-    built = 0
-
-    def tables_step(count):
-        nonlocal built
-        for o in range(built, min(built + count, observers)):
+    waiting = list(stored)
+    for c in range(len(SHARES)):
+        for o in waiting[:len(stored) * TABLES[c] // sum(TABLES)]:
             table_step(o)
-        built = min(built + count, observers)
-
-    tables_step(TABLES[0])
-    for c in range(len(SHARES)):
+            waiting.remove(o)
         greens[c].wait()
         loads[c].wait()
         for tile in range(edges[c], edges[c + 1]):
             widen_step(tile)
             spread_step(0, observers, tile)
-        tables_step(TABLES[c + 1] if c + 1 < len(SHARES) else observers)
+    for o in waiting:
+        table_step(o)
 
     for c in range(len(spans)):
         for first in range(spans[c][0], spans[c][1], ROWS):

time: 14 us -> 13.7 us (0.979)
  Pallas kernels: 13.2 us -> 13 us
    pallas_call x1, Pallas kernels: 13.2 us -> 13 us  [shards(): pl.pallas_call(functools.partial(kernel, panels, slabs), out_shape=jax.Sh...]
where the time goes in v3:
time: 13.7 us; the launch traced here: 13.6 us
  Pallas kernels  13 us (95%)
  local copies, waits for them, and re-layouts  0.62 us (5%)
    pallas_call x1, Pallas kernels, shards(): pl.pallas_call(functools.partial(kernel, panels, slabs), out_shape=jax.Sh...  13 us
    unnamed x1, local copies, waits for them, and re-layouts  0.62 us

profile of v3, /device:TPU:0, one launch (start us, length us, event | category | flops | bytes accessed | tf_op | source)
XLA Modules:
  0.0 13.6 jit_solution(11571920727090834007)
XLA Ops:
  0.0 13.0 %far_field.1 = f32[32,256]{1,0:T(8,128)S(1)} custom-call(s32[4]{0:T(128)} %live_hbm.1, bf16[8192,256]{1,0:T(8,128)(2,1)} %load_hbm.1, bf16[32,8192]{1,0:T(8,128)(2,1)} %green_hbm.1, s32[32,512]{1,0:T(8,128)} %delay_hbm.1, s32[32,512]{1,0:T(8,128)} %offset_hbm.1), custom_call_target="tpu_custom_call" | custom-call | tf_op jit(solution)/shard_map/far_field/pallas_call | solution.py:281
  13.0 0.6 %copy.7 = f32[32,256]{1,0:T(8,128)} copy(f32[32,256]{1,0:T(8,128)S(1)} %far_field.1) | data formatting | bytes 65536

commit v4 on v3

--- a/solution.py
+++ b/solution.py
@@ -18,7 +18,6 @@
 ROWS = 8
 SHARES = (4, 12, 16)
 TABLES = (1, 1, 1, 1)
-EVERY = 99
 LATE = 8
 MESH = pl.DeviceIdType.MESH
 
@@ -90,7 +89,7 @@
     delay_ref[...] = jnp.where(group_of < live, delay_ref[...], 4 * LAGS)
     offset_ref[...] = offset_ref[...] * TAPS
 
-    stored = [o for o in range(observers) if o >= observers - LATE or o % EVERY == 0]
+    stored = [o for o in range(observers) if o == 0 or o >= observers - LATE]
 
     def entries(o, a):
         lanes = slice(a * LANES, (a + 1) * LANES)
@@ -186,7 +185,7 @@
             bit //= 2
         return folded[0]
 
-    spans = ((0, observers - LATE), (observers - LATE, observers))
+    spans = ((0, observers),)
 
     def main_copy(c, d):
         rows = slice(*spans[c])

time: 13.7 us -> 13.5 us (0.985)
  Pallas kernels: 13 us -> 12.7 us
    pallas_call x1, Pallas kernels: 13 us -> 12.7 us  [shards(): pl.pallas_call(functools.partial(kernel, panels, slabs), out_shape=jax.Sh...]
where the time goes in v4:
time: 13.5 us; the launch traced here: 13.3 us
  Pallas kernels  12.7 us (94%)
  local copies, waits for them, and re-layouts  0.62 us (5%)
    pallas_call x1, Pallas kernels, shards(): pl.pallas_call(functools.partial(kernel, panels, slabs), out_shape=jax.Sh...  12.7 us
    unnamed x1, local copies, waits for them, and re-layouts  0.62 us

profile of v4, /device:TPU:0, one launch (start us, length us, event | category | flops | bytes accessed | tf_op | source)
XLA Modules:
  0.0 13.3 jit_solution(3310028137455022962)
XLA Ops:
  0.0 12.7 %far_field.1 = f32[32,256]{1,0:T(8,128)S(1)} custom-call(s32[4]{0:T(128)} %live_hbm.1, bf16[8192,256]{1,0:T(8,128)(2,1)} %load_hbm.1, bf16[32,8192]{1,0:T(8,128)(2,1)} %green_hbm.1, s32[32,512]{1,0:T(8,128)} %delay_hbm.1, s32[32,512]{1,0:T(8,128)} %offset_hbm.1), custom_call_target="tpu_custom_call" | custom-call | tf_op jit(solution)/shard_map/far_field/pallas_call | solution.py:280
  12.7 0.6 %copy.7 = f32[32,256]{1,0:T(8,128)} copy(f32[32,256]{1,0:T(8,128)S(1)} %far_field.1) | data formatting | bytes 65536

commit v5 on v4

--- a/solution.py
+++ b/solution.py
@@ -177,13 +177,10 @@
             move.append(jnp.where(clear, pltpu.roll(a, ROWS - bit, 0), b))
         return add(shift(move, bit), stay)
 
-    def gather(folded):
-        bit = ROWS // 2
-        while len(folded) > 1:
-            half = len(folded) // 2
-            folded = [merge(folded[i], folded[i + half], bit) for i in range(half)]
-            bit //= 2
-        return folded[0]
+    def gather(first, bit):
+        if bit == ROWS // 2:
+            return merge(*fold(lag_step(first), lag_step(first + bit)), bit)
+        return merge(gather(first, 2 * bit), gather(first + bit, 2 * bit), bit)
 
     spans = ((0, observers),)
 
@@ -204,10 +201,7 @@
             device_id={"panel": lax.rem(panel + d, panels), "slab": slab + 1}, device_id_type=MESH)
 
     def sum_rows(first):
-        folded = []
-        for o in range(first, first + ROWS, 2):
-            folded += fold(lag_step(o), lag_step(o + 1))
-        gathered = gather(folded)
+        gathered = gather(first, 1)
         rows = slice(first, first + ROWS)
         for j in range(wide):
             lanes = slice(j * LANES, (j + 1) * LANES)

time: 13.5 us -> 13.5 us (level)
  no operation moved by 1% of the time
where the time goes in v5:
time: 13.5 us; the launch traced here: 13.3 us
  Pallas kernels  12.7 us (94%)
  local copies, waits for them, and re-layouts  0.62 us (5%)
    pallas_call x1, Pallas kernels, shards(): pl.pallas_call(functools.partial(kernel, panels, slabs), out_shape=jax.Sh...  12.7 us
    unnamed x1, local copies, waits for them, and re-layouts  0.62 us

profile of v5, /device:TPU:0, one launch (start us, length us, event | category | flops | bytes accessed | tf_op | source)
XLA Modules:
  0.0 13.3 jit_solution(4685801366360787790)
XLA Ops:
  0.0 12.7 %far_field.1 = f32[32,256]{1,0:T(8,128)S(1)} custom-call(s32[4]{0:T(128)} %live_hbm.1, bf16[8192,256]{1,0:T(8,128)(2,1)} %load_hbm.1, bf16[32,8192]{1,0:T(8,128)(2,1)} %green_hbm.1, s32[32,512]{1,0:T(8,128)} %delay_hbm.1, s32[32,512]{1,0:T(8,128)} %offset_hbm.1), custom_call_target="tpu_custom_call" | custom-call | tf_op jit(solution)/shard_map/far_field/pallas_call | solution.py:274
  12.7 0.6 %copy.7 = f32[32,256]{1,0:T(8,128)} copy(f32[32,256]{1,0:T(8,128)S(1)} %far_field.1) | data formatting | bytes 65536
